TPU v7x, 32 devices: a whole 2x2x4 slice. The times are simulated.
32 devices in a mesh: dp: 4 (over x, core), tensor: 8 (over z, y).
Axes of the slice: x: 2, y: 2, z: 4, core: 2. Of those that a mesh axis runs over, the one named last changes fastest.
Arguments:
- hidden: bfloat16 [3072, 4096], P('dp', 'tensor'), may hold values from -2000 to 2000
- out_embed: bfloat16 [16384, 4096], P('tensor', 'dp'), may hold values from -0.3 to 0.3
- labels: int32 [3072], P('dp'), may hold values from 0 to 16383
Outputs:
- token_loss: float32 [3072], P(('dp', 'tensor'))
- mean_loss: float32 [], replicated
All inputs are finite; a program needn't handle non-finite values.
Results may differ from a plain program's by a relative error of at most 0.0003.
Values may be sent and summed in bfloat16 or wider, within the bound.
No kernel may reach another device: no remote copies, remote signals or barrier semaphores. Data moves between devices by JAX's collectives and lax.ppermute only.
A program may use at most 128 MiB of HBM per device.

v0:
```python
import jax
import jax.numpy as jnp
from jax import lax
from jax.sharding import PartitionSpec as P

BLOCK = 512


def combine_stats(first, second):
    peak_first, mass_first, label_first = first
    peak_second, mass_second, label_second = second
    peak_value = jnp.maximum(peak_first, peak_second)
    exp_total = mass_first * jnp.exp(peak_first - peak_value) + mass_second * jnp.exp(
        peak_second - peak_value
    )
    return (peak_value, exp_total, label_first + label_second)


def block_stats(logits, first_row, labels):
    peak_value = jnp.max(logits, axis=0)
    exp_total = jnp.sum(jnp.exp(logits - peak_value[None, :]), axis=0)
    row_ids = first_row + lax.broadcasted_iota(jnp.int32, logits.shape, 0)
    label_logit = jnp.sum(
        jnp.where(row_ids == labels[None, :], logits, jnp.zeros_like(logits)), axis=0
    )
    return (peak_value, exp_total, label_logit)


def body(hidden, out_embed, labels):
    full_hidden = lax.all_gather(hidden, "tensor", axis=1, tiled=True)
    token_count = full_hidden.shape[0]
    vocab_rows = out_embed.shape[0]
    vocab_offset = lax.axis_index("tensor") * vocab_rows
    block_count = vocab_rows // BLOCK
    running_stats = None
    for block_index in range(block_count):
        weight_block = out_embed[block_index * BLOCK : (block_index + 1) * BLOCK]
        stats = block_stats(
            lax.dot_general(
                lax.all_gather(weight_block, "dp", axis=1, tiled=True),
                full_hidden,
                (((1,), (1,)), ((), ())),
                preferred_element_type=jnp.float32,
            ),
            vocab_offset + block_index * BLOCK,
            labels,
        )
        running_stats = stats if running_stats is None else combine_stats(running_stats, stats)
    groups = lax.axis_size("tensor")
    share = token_count // groups
    peak_all, mass_all, label_all = running_stats
    peaks, masses, picked = (
        lax.all_to_all(
            peak_all.reshape(groups, share), "tensor", split_axis=0, concat_axis=0, tiled=True
        ),
        lax.all_to_all(
            mass_all.reshape(groups, share), "tensor", split_axis=0, concat_axis=0, tiled=True
        ),
        lax.all_to_all(
            label_all.reshape(groups, share), "tensor", split_axis=0, concat_axis=0, tiled=True
        ),
    )
    peak_value = jnp.max(peaks, axis=0)
    exp_total = jnp.sum(masses * jnp.exp(peaks - peak_value[None, :]), axis=0)
    label_logit = jnp.sum(picked, axis=0)
    token_loss = jnp.log(exp_total) + peak_value - label_logit
    loss_sum = lax.psum(jnp.sum(token_loss), ("dp", "tensor"))
    mean_loss = loss_sum / (share * lax.axis_size("dp") * groups)
    return (token_loss, mean_loss)


def solution(mesh):
    return jax.shard_map(
        body,
        mesh=mesh,
        in_specs=(P("dp", "tensor"), P("tensor", "dp"), P("dp")),
        out_specs=(P(("dp", "tensor")), P()),
        check_vma=False,
    )
```

profile of v0, /device:TPU:0, one launch (start us, length us, event | category | flops | bytes accessed | tf_op | source)
XLA Modules:
  0.0 347.8 jit_solution(11114172861355873410)
XLA Ops:
  7.2 0.0 all-gather.6.cloned.1.call-start
  7.2 4.2 %fusion.2 = (bf16[512,1024]{1,0:T(8,128)(2,1)}, bf16[512,1024]{1,0:T(8,128)(2,1)}, bf16[512,1024]{1,0:T(8,128)(2,1)}, bf16[512,1024]{1,0:T(8,128)(2,1)}) fusion(bf16[2048,1024]{1,0:T(8,128)(2,1)} %param.4), kind=kLoop, calls=%fused_computation.18 | loop fusion | bytes 8388608 | tf_op jit(solution)/shard_map/slice | solution.py:37
  11.5 0.0 all-gather.6.cloned.1.call-update
  11.5 0.0 all-gather.8.cloned.1.call-start
  11.5 0.7 all-gather.8.cloned.1.call-update
  12.2 0.0 all-gather.10.cloned.1.call-start
  12.3 0.7 all-gather.10.cloned.1.call-update
  13.0 0.0 all-gather.12.cloned.1.call-start
  13.0 0.5 all-gather.12.cloned.1.call-update
  13.5 0.0 all-gather.14.cloned.1.call-start
  13.6 0.5 all-gather.14.cloned.1.call-update
  14.2 34.7 %all-gather.6.cloned.1.call-done = bf16[512,4096]{1,0:T(8,128)(2,1)} async-done(((bf16[512,1024]{1,0:T(8,128)(2,1)}), bf16[512,4096]{1,0:T(8,128)(2,1)}) %all-gather.6.cloned.1.call-update) | async-done | bytes 4194320 | tf_op jit(solution)/shard_map/all_gather | solution.py:40
  48.8 101.6 %all-gather.8.cloned.1.call-done = bf16[768,4096]{1,0:T(8,128)(2,1)} async-done(((bf16[768,512]{1,0:T(8,128)(2,1)}), bf16[768,4096]{1,0:T(8,128)(2,1)}) %all-gather.8.cloned.1.call-update) | async-done | bytes 6291472 | tf_op jit(solution)/shard_map/all_gather | solution.py:30
  150.4 7.1 %fusion.6 = (f32[768]{0:T(1024)S(1)}, f32[512,768]{1,0:T(8,128)S(1)}) fusion(bf16[512,4096]{1,0:T(8,128)(2,1)} %all-gather.6.cloned.1.call-done, bf16[768,4096]{1,0:T(8,128)(2,1)} %all-gather.8.cloned.1.call-done), kind=kOutput, calls=%fused_computation.22 | convolution fusion | flops 3221617920 | bytes 12061696 | tf_op jit(solution)/shard_map/dot_general | solution.py:39
  157.5 0.1 reduce_max.54
  157.6 27.0 %all-gather.10.cloned.1.call-done = bf16[512,4096]{1,0:T(8,128)(2,1)} async-done(((bf16[512,1024]{1,0:T(8,128)(2,1)}), bf16[512,4096]{1,0:T(8,128)(2,1)}) %all-gather.10.cloned.1.call-update) | async-done | bytes 4194320 | tf_op jit(solution)/shard_map/all_gather | solution.py:40
  184.6 7.1 %fusion.3 = (f32[768]{0:T(1024)S(1)}, f32[512,768]{1,0:T(8,128)S(1)}) fusion(bf16[512,4096]{1,0:T(8,128)(2,1)} %all-gather.10.cloned.1.call-done, bf16[768,4096]{1,0:T(8,128)(2,1)} %all-gather.8.cloned.1.call-done), kind=kOutput, calls=%fused_computation.19 | convolution fusion | flops 3221617920 | bytes 12061696 | tf_op jit(solution)/shard_map/dot_general | solution.py:39
  191.7 0.1 reduce_max.56
  191.8 28.7 %all-gather.12.cloned.1.call-done = bf16[512,4096]{1,0:T(8,128)(2,1)} async-done(((bf16[512,1024]{1,0:T(8,128)(2,1)}), bf16[512,4096]{1,0:T(8,128)(2,1)}) %all-gather.12.cloned.1.call-update) | async-done | bytes 4194320 | tf_op jit(solution)/shard_map/all_gather | solution.py:40
  220.5 8.7 %fusion.4 = (f32[768]{0:T(1024)S(1)}, f32[512,768]{1,0:T(8,128)}) fusion(bf16[512,4096]{1,0:T(8,128)(2,1)} %all-gather.12.cloned.1.call-done, bf16[768,4096]{1,0:T(8,128)(2,1)} %all-gather.8.cloned.1.call-done), kind=kOutput, calls=%fused_computation.20 | convolution fusion | flops 3221617920 | bytes 12061696 | tf_op jit(solution)/shard_map/dot_general | solution.py:39
  229.2 0.1 reduce_max.58
  229.3 0.0 copy-start
  229.3 27.1 %all-gather.14.cloned.1.call-done = bf16[512,4096]{1,0:T(8,128)(2,1)} async-done(((bf16[512,1024]{1,0:T(8,128)(2,1)}), bf16[512,4096]{1,0:T(8,128)(2,1)}) %all-gather.14.cloned.1.call-update) | async-done | bytes 4194320 | tf_op jit(solution)/shard_map/all_gather | solution.py:40
  256.4 8.7 %fusion.5 = (f32[768]{0:T(1024)S(1)}, f32[512,768]{1,0:T(8,128)}) fusion(bf16[512,4096]{1,0:T(8,128)(2,1)} %all-gather.14.cloned.1.call-done, bf16[768,4096]{1,0:T(8,128)(2,1)} %all-gather.8.cloned.1.call-done), kind=kOutput, calls=%fused_computation.21 | convolution fusion | flops 3221617920 | bytes 12061696 | tf_op jit(solution)/shard_map/dot_general | solution.py:39
  265.1 0.1 reduce_max.60
  265.1 0.0 copy-done
  265.1 3.2 exponential_reduce_fusion.2
  268.4 0.1 reduce_sum.108
  268.4 0.1 reduce_sum.110
  268.5 0.1 reduce_sum.112
  268.6 0.1 reduce_sum.114
  268.7 0.6 multiply_add_fusion
  269.3 5.5 %all-to-all-start.1 = ((f32[8,1,96]{2,1,0:T(1,128)}), f32[8,1,96]{2,1,0:T(1,128)S(1)}, u32[]{:S(2)}, u32[]{:S(2)}) async-start(f32[8,1,96]{2,1,0:T(1,128)} %bitcast.2), calls=%async_computation.1 | async-start | bytes 8192 | tf_op jit(solution)/shard_map/all_to_all | solution.py:53
  274.8 0.1 add.131
  274.9 6.4 %all-to-all-done.1 = f32[8,1,96]{2,1,0:T(1,128)S(1)} async-done(((f32[8,1,96]{2,1,0:T(1,128)}), f32[8,1,96]{2,1,0:T(1,128)S(1)}, u32[]{:S(2)}, u32[]{:S(2)}) %all-to-all-start.1) | async-done | bytes 3104 | tf_op jit(solution)/shard_map/all_to_all | solution.py:53
  281.3 8.8 %all_to_all.24 = f32[8,1,96]{2,1,0:T(1,128)S(1)} all-to-all(f32[8,1,96]{2,1,0:T(1,128)S(1)} %add.131), channel_id=1, replica_groups=mesh['dp'=4,'tensor'=8] {'tensor'}, dimensions={0} | all-to-all | bytes 6144 | tf_op jit(solution)/shard_map/all_to_all | solution.py:59
  290.1 3.3 all-to-all-start
  293.5 6.4 %all-to-all-done = f32[8,1,96]{2,1,0:T(1,128)S(1)} async-done(((f32[8,1,96]{2,1,0:T(1,128)}), f32[8,1,96]{2,1,0:T(1,128)S(1)}, u32[]{:S(2)}, u32[]{:S(2)}) %all-to-all-start) | async-done | bytes 3104 | tf_op jit(solution)/shard_map/all_to_all | solution.py:56
  299.9 1.1 fusion
  301.0 38.4 %psum.7 = f32[]{:T(128)} all-reduce(f32[]{:T(128)} %get-tuple-element.10), channel_id=1, replica_groups=mesh['dp'=4,'tensor'=8] {'dp','tensor'}, use_global_device_ids=true, to_apply=%region_16.17 | all-reduce | flops 1 | bytes 8 | tf_op jit(solution)/shard_map/psum | solution.py:67
  (7 shorter events, 0.1 us)
Async XLA Ops:
  7.2 41.6 %all-gather.6.cloned.1.call-start = ((), (), s32[]{:S(2)}) async-start(), calls=%async_computation.3 | async-start | bytes 5242880 | tf_op jit(solution)/shard_map/all_gather | solution.py:40
  11.5 138.9 %all-gather.8.cloned.1.call-start = ((), (), s32[]{:S(2)}) async-start(), calls=%async_computation.4 | async-start | bytes 7077888 | tf_op jit(solution)/shard_map/all_gather | solution.py:30
  12.2 172.4 %all-gather.10.cloned.1.call-start = ((), (), s32[]{:S(2)}) async-start(), calls=%async_computation.5 | async-start | bytes 5242880 | tf_op jit(solution)/shard_map/all_gather | solution.py:40
  13.0 207.5 %all-gather.12.cloned.1.call-start = ((), (), s32[]{:S(2)}) async-start(), calls=%async_computation.6 | async-start | bytes 5242880 | tf_op jit(solution)/shard_map/all_gather | solution.py:40
  13.5 242.9 %all-gather.14.cloned.1.call-start = ((), (), s32[]{:S(2)}) async-start(), calls=%async_computation.7 | async-start | bytes 5242880 | tf_op jit(solution)/shard_map/all_gather | solution.py:40
  229.3 35.9 %copy-start = (s32[768]{0:T(1024)S(1)}, s32[768]{0:T(1024)}, u32[]{:S(2)}) copy-start(s32[768]{0:T(1024)} %param.5) | copy-start | bytes 9220
  269.3 12.0 %all-to-all-start.1 = ((f32[8,1,96]{2,1,0:T(1,128)}), f32[8,1,96]{2,1,0:T(1,128)S(1)}, u32[]{:S(2)}, u32[]{:S(2)}) async-start(f32[8,1,96]{2,1,0:T(1,128)} %bitcast.2), calls=%async_computation.1 | async-start | bytes 8192 | tf_op jit(solution)/shard_map/all_to_all | solution.py:53
  290.1 9.8 %all-to-all-start = ((f32[8,1,96]{2,1,0:T(1,128)}), f32[8,1,96]{2,1,0:T(1,128)S(1)}, u32[]{:S(2)}, u32[]{:S(2)}) async-start(f32[8,1,96]{2,1,0:T(1,128)} %bitcast), calls=%async_computation | async-start | bytes 8192 | tf_op jit(solution)/shard_map/all_to_all | solution.py:56
Sparse Core Ops, SparseCore 0:
  11.6 37.1 all-gather.5
  50.9 99.4 all-gather.7
  151.9 32.6 all-gather.9
  186.0 34.4 all-gather.11
  221.9 34.4 all-gather.13
where the time goes:
time: 348 us
  waiting for transfers between devices  234 us (67%)
  blocking collectives  47.2 us (14%)
  matrix products  31.6 us (9%)
  between operations  15.6 us (4%)
  starting transfers between devices  9.04 us (3%)
  other arithmetic  5.05 us (1%)
  local copies, waits for them, and re-layouts  4.9 us (1%)
    all_gather x4, waiting for transfers between devices, body(): lax.all_gather(weight_block, 'dp', axis=1, tiled=True)  118 us
    all_gather x1, waiting for transfers between devices, body(): full_hidden = lax.all_gather(hidden, 'tensor', axis=1, tiled=True)  102 us
    psum x1, blocking collectives, body(): loss_sum = lax.psum(jnp.sum(token_loss), ('dp', 'tensor'))  38.4 us
    dot_general x4, matrix products, body(): lax.dot_general(lax.all_gather(weight_block, 'dp', axis=1, tiled=True), f...  31.6 us
    all_to_all x1, blocking collectives, body(): lax.all_to_all(label_all.reshape(groups, share), 'tensor', split_axis=0,...  8.85 us
  transfers between devices with their start and end apart: 7, of which 7 were waited for; matrix products, arithmetic and copies ran while one was open for 7% of the time, Pallas kernels for 0%

commit v1 on v0

--- a/solution.py
+++ b/solution.py
@@ -4,6 +4,18 @@
 from jax.sharding import PartitionSpec as P
 
 BLOCK = 512
+
+
+def doubled_up(x, axis, dim):
+    ways, here = (lax.axis_size(axis), lax.axis_index(axis))
+    grown, reach = (x, 1)
+    while reach < ways:
+        theirs = lax.ppermute(grown, axis, [(d, d ^ reach) for d in range(ways)])
+        mine_first = jnp.concatenate([grown, theirs], axis=dim)
+        theirs_first = jnp.concatenate([theirs, grown], axis=dim)
+        grown = jnp.where(here & reach == 0, mine_first, theirs_first)
+        reach = 2 * reach
+    return grown
 
 
 def combine_stats(first, second):
@@ -37,7 +49,7 @@
         weight_block = out_embed[block_index * BLOCK : (block_index + 1) * BLOCK]
         stats = block_stats(
             lax.dot_general(
-                lax.all_gather(weight_block, "dp", axis=1, tiled=True),
+                doubled_up(weight_block, "dp", 1),
                 full_hidden,
                 (((1,), (1,)), ((), ())),
                 preferred_element_type=jnp.float32,

time: 348 us -> 306 us (0.88)
  waiting for transfers between devices: 234 us -> 165 us
  other arithmetic: 5.05 us -> 19.3 us
  matrix products: 31.6 us -> 38.8 us
  starting transfers between devices: 9.04 us -> 15.4 us
    all_gather x4 -> x0, waiting for transfers between devices: 118 us -> none  [body(): lax.all_gather(weight_block, 'dp', axis=1, tiled=True)]
    ppermute x0 -> x8, waiting for transfers between devices: none -> 108 us  [doubled_up(): theirs = lax.ppermute(grown, axis, [(d, d ^ reach) for d in range(ways)])]
    all_gather x1, waiting for transfers between devices: 102 us -> 43.3 us  [body(): full_hidden = lax.all_gather(hidden, 'tensor', axis=1, tiled=True)]
    select_n x0 -> x4, other arithmetic: none -> 14.3 us  [doubled_up(): grown = jnp.where(here & reach == 0, mine_first, theirs_first)]
    dot_general x4, matrix products: 31.6 us -> 38.8 us  [body(): lax.dot_general(doubled_up(weight_block, 'dp', 1), full_hidden, (((1,), (...]
    ppermute x0 -> x8, starting transfers between devices: none -> 5.96 us  [doubled_up(): theirs = lax.ppermute(grown, axis, [(d, d ^ reach) for d in range(ways)])]
  transfers between devices with their start and end apart: 7 -> 11, of which waited for: 7 -> 6; matrix products, arithmetic and copies ran while one was open for 7% -> 15% of each run, Pallas kernels for 0% -> 0%
where the time goes in v1:
time: 306 us
  waiting for transfers between devices  165 us (54%)
  blocking collectives  47.3 us (15%)
  matrix products  38.8 us (13%)
  other arithmetic  19.3 us (6%)
  between operations  15.9 us (5%)
  starting transfers between devices  15.4 us (5%)
  local copies, waits for them, and re-layouts  4.52 us (1%)
    ppermute x8, waiting for transfers between devices, doubled_up(): theirs = lax.ppermute(grown, axis, [(d, d ^ reach) for d in range(ways)])  108 us
    all_gather x1, waiting for transfers between devices, body(): full_hidden = lax.all_gather(hidden, 'tensor', axis=1, tiled=True)  43.3 us
    dot_general x4, matrix products, body(): lax.dot_general(doubled_up(weight_block, 'dp', 1), full_hidden, (((1,), (...  38.8 us
    psum x1, blocking collectives, body(): loss_sum = lax.psum(jnp.sum(token_loss), ('dp', 'tensor'))  38.5 us
    select_n x4, other arithmetic, doubled_up(): grown = jnp.where(here & reach == 0, mine_first, theirs_first)  14.3 us
    all_to_all x1, blocking collectives, body(): lax.all_to_all(label_all.reshape(groups, share), 'tensor', split_axis=0,...  8.85 us
    all_to_all x1, waiting for transfers between devices, body(): lax.all_to_all(peak_all.reshape(groups, share), 'tensor', split_axis=0, c...  6.4 us
    all_to_all x1, waiting for transfers between devices, body(): lax.all_to_all(mass_all.reshape(groups, share), 'tensor', split_axis=0, c...  6.38 us
  transfers between devices with their start and end apart: 11, of which 6 were waited for; matrix products, arithmetic and copies ran while one was open for 15% of the time, Pallas kernels for 0%

profile of v1, /device:TPU:0, one launch (start us, length us, event | category | flops | bytes accessed | tf_op | source)
XLA Modules:
  0.0 305.8 jit_solution(17577606705843589255)
XLA Ops:
  7.2 0.0 all-gather.2.cloned.1.call-start
  7.2 0.7 all-gather.2.cloned.1.call-update
  7.9 3.9 %fusion.34 = (bf16[512,1024]{1,0:T(8,128)(2,1)S(1)}, bf16[512,1024]{1,0:T(8,128)(2,1)}, bf16[512,1024]{1,0:T(8,128)(2,1)S(1)}, bf16[512,1024]{1,0:T(8,128)(2,1)S(1)}) fusion(bf16[2048,1024]{1,0:T(8,128)(2,1)} %param.4), kind=kLoop, calls=%fused_computation.58 | loop fusion | bytes 8388608 | tf_op jit(solution)/shard_map/slice | solution.py:49
  11.8 0.5 collective-permute-start
  12.2 0.0 collective-permute-start.4
  12.3 2.6 collective-permute-done
  14.9 4.4 %maximum_select_fusion.8 = bf16[512,2048]{1,0:T(8,128)(2,1)} fusion(bf16[512,1024]{1,0:T(8,128)(2,1)} %collective-permute-done, bf16[512,1024]{1,0:T(8,128)(2,1)} %get-tuple-element.17, pred[]{:T(512)S(6)} %eq.15), kind=kLoop, calls=%fused_computation.32 | loop fusion | flops 9437184 | bytes 4194305 | tf_op jit(solution)/shard_map/jit(_where)/select_n | solution.py:16
  19.3 2.8 collective-permute-start.1
  22.2 0.0 collective-permute-start.6
  22.2 0.5 collective-permute-start.2
  22.7 0.0 collective-permute-done.4
  22.7 3.8 %maximum_select_fusion.10 = bf16[512,2048]{1,0:T(8,128)(2,1)} fusion(bf16[512,1024]{1,0:T(8,128)(2,1)} %collective-permute-done.4, bf16[512,1024]{1,0:T(8,128)(2,1)S(1)} %get-tuple-element.19, pred[]{:T(512)S(6)} %eq.15), kind=kLoop, calls=%fused_computation.34 | loop fusion | flops 9437184 | bytes 4194305 | tf_op jit(solution)/shard_map/jit(_where)/select_n | solution.py:16
  26.5 0.0 collective-permute-start.5
  26.5 0.0 collective-permute-done.6
  26.5 3.7 %maximum_select_fusion.11 = bf16[512,2048]{1,0:T(8,128)(2,1)} fusion(bf16[512,1024]{1,0:T(8,128)(2,1)} %collective-permute-done.6, bf16[512,1024]{1,0:T(8,128)(2,1)S(1)} %get-tuple-element.18, pred[]{:T(512)S(6)} %eq.15), kind=kLoop, calls=%fused_computation.35 | loop fusion | flops 9437184 | bytes 4194305 | tf_op jit(solution)/shard_map/jit(_where)/select_n | solution.py:16
  30.2 2.0 collective-permute-start.7
  32.2 0.0 collective-permute-done.2
  32.2 2.3 maximum_select_fusion.9
  34.6 0.1 collective-permute-start.3
  34.7 34.3 %collective-permute-done.1 = bf16[512,2048]{1,0:T(8,128)(2,1)} collective-permute-done((bf16[512,2048]{1,0:T(8,128)(2,1)}, bf16[512,2048]{1,0:T(8,128)(2,1)}, u32[]{:S(2)}, u32[]{:S(2)}) %collective-permute-start.1) | collective-permute-done | bytes 2097184 | tf_op jit(solution)/shard_map/ppermute | solution.py:13
  69.0 43.3 %all-gather.2.cloned.1.call-done = bf16[768,4096]{1,0:T(8,128)(2,1)} async-done(((bf16[768,512]{1,0:T(8,128)(2,1)}), bf16[768,4096]{1,0:T(8,128)(2,1)}) %all-gather.2.cloned.1.call-update) | async-done | bytes 6291472 | tf_op jit(solution)/shard_map/all_gather | solution.py:42
  112.3 9.9 %fusion.38 = (f32[768]{0:T(1024)S(1)}, f32[512,768]{1,0:T(8,128)}) fusion(bf16[768,4096]{1,0:T(8,128)(2,1)} %all-gather.2.cloned.1.call-done, bf16[512,2048]{1,0:T(8,128)(2,1)} %collective-permute-done.1, bf16[512,2048]{1,0:T(8,128)(2,1)} %maximum_select_fusion.8, pred[]{:T(512)S(6)} %eq.14), kind=kOutput, calls=%fused_computation.62 | convolution fusion | flops 3240492288 | bytes 12061697 | tf_op jit(solution)/shard_map/dot_general | solution.py:51
  122.2 0.1 reduce_max.54
  122.2 0.0 collective-permute-done.5
  122.2 10.0 %fusion.36 = (f32[768]{0:T(1024)S(1)}, f32[512,768]{1,0:T(8,128)}) fusion(bf16[768,4096]{1,0:T(8,128)(2,1)} %all-gather.2.cloned.1.call-done, bf16[512,2048]{1,0:T(8,128)(2,1)} %collective-permute-done.5, bf16[512,2048]{1,0:T(8,128)(2,1)} %maximum_select_fusion.10, pred[]{:T(512)S(6)} %eq.14), kind=kOutput, calls=%fused_computation.60 | convolution fusion | flops 3240492288 | bytes 12061697 | tf_op jit(solution)/shard_map/dot_general | solution.py:51
  132.2 0.1 reduce_max.58
  132.3 71.0 %collective-permute-done.3 = bf16[512,2048]{1,0:T(8,128)(2,1)} collective-permute-done((bf16[512,2048]{1,0:T(8,128)(2,1)S(1)}, bf16[512,2048]{1,0:T(8,128)(2,1)}, u32[]{:S(2)}, u32[]{:S(2)}) %collective-permute-start.3) | collective-permute-done | bytes 2097184 | tf_op jit(solution)/shard_map/ppermute | solution.py:13
  203.2 8.9 %fusion.35 = (f32[768]{0:T(1024)S(1)}, f32[512,768]{1,0:T(8,128)}) fusion(bf16[768,4096]{1,0:T(8,128)(2,1)} %all-gather.2.cloned.1.call-done, bf16[512,2048]{1,0:T(8,128)(2,1)} %collective-permute-done.3, bf16[512,2048]{1,0:T(8,128)(2,1)S(1)} %maximum_select_fusion.9, pred[]{:T(512)S(6)} %eq.14), kind=kOutput, calls=%fused_computation.59 | convolution fusion | flops 3240492288 | bytes 12061697 | tf_op jit(solution)/shard_map/dot_general | solution.py:51
  212.1 0.1 reduce_max.56
  212.2 0.0 copy-start
  212.2 0.0 copy-start.1
  212.2 0.0 copy-start.2
  212.2 0.0 collective-permute-done.7
  212.2 10.0 %fusion.37 = (f32[768]{0:T(1024)S(1)}, f32[512,768]{1,0:T(8,128)}) fusion(bf16[768,4096]{1,0:T(8,128)(2,1)} %all-gather.2.cloned.1.call-done, bf16[512,2048]{1,0:T(8,128)(2,1)} %collective-permute-done.7, bf16[512,2048]{1,0:T(8,128)(2,1)} %maximum_select_fusion.11, pred[]{:T(512)S(6)} %eq.14), kind=kOutput, calls=%fused_computation.61 | convolution fusion | flops 3240492288 | bytes 12061697 | tf_op jit(solution)/shard_map/dot_general | solution.py:51
  222.2 0.1 reduce_max.60
  222.3 0.0 copy-done
  222.3 0.0 copy-done.1
  222.3 0.0 copy-done.2
  222.3 3.1 %exponential_reduce_fusion.2 = (f32[768]{0:T(1024)S(1)}, f32[768]{0:T(1024)S(1)}, f32[768]{0:T(1024)S(1)}, f32[768]{0:T(1024)S(1)}, f32[768]{0:T(1024)S(1)}, /*i...) fusion(f32[512,768]{1,0:T(8,128)} %get-tuple-element.27, f32[768]{0:T(1024)S(1)} %get-tuple-element.26, ...), kind=kLoop, calls=%fused_computation.42 | loop fusion | flops 7858176 | bytes 6339584 | tf_op jit(solution)/shard_map/reduce_sum | solution.py:33
  225.5 0.1 reduce_sum.108
  225.5 0.1 reduce_sum.110
  225.6 0.1 reduce_sum.112
  225.7 0.1 reduce_sum.114
  225.8 0.6 multiply_add_fusion
  226.4 6.1 %all-to-all-start.1 = ((f32[8,1,96]{2,1,0:T(1,128)}), f32[8,1,96]{2,1,0:T(1,128)S(1)}, u32[]{:S(2)}, u32[]{:S(2)}) async-start(f32[8,1,96]{2,1,0:T(1,128)} %bitcast.2), calls=%async_computation.1 | async-start | bytes 8192 | tf_op jit(solution)/shard_map/all_to_all | solution.py:65
  232.5 0.1 add.131
  232.5 6.4 %all-to-all-done.1 = f32[8,1,96]{2,1,0:T(1,128)S(1)} async-done(((f32[8,1,96]{2,1,0:T(1,128)}), f32[8,1,96]{2,1,0:T(1,128)S(1)}, u32[]{:S(2)}, u32[]{:S(2)}) %all-to-all-start.1) | async-done | bytes 3104 | tf_op jit(solution)/shard_map/all_to_all | solution.py:65
  238.9 8.8 %all_to_all.24 = f32[8,1,96]{2,1,0:T(1,128)S(1)} all-to-all(f32[8,1,96]{2,1,0:T(1,128)S(1)} %add.131), channel_id=1, replica_groups=mesh['dp'=4,'tensor'=8] {'tensor'}, dimensions={0} | all-to-all | bytes 6144 | tf_op jit(solution)/shard_map/all_to_all | solution.py:71
  247.8 3.3 %all-to-all-start = ((f32[8,1,96]{2,1,0:T(1,128)}), f32[8,1,96]{2,1,0:T(1,128)S(1)}, u32[]{:S(2)}, u32[]{:S(2)}) async-start(f32[8,1,96]{2,1,0:T(1,128)} %bitcast), calls=%async_computation | async-start | bytes 8192 | tf_op jit(solution)/shard_map/all_to_all | solution.py:68
  251.2 6.4 %all-to-all-done = f32[8,1,96]{2,1,0:T(1,128)S(1)} async-done(((f32[8,1,96]{2,1,0:T(1,128)}), f32[8,1,96]{2,1,0:T(1,128)S(1)}, u32[]{:S(2)}, u32[]{:S(2)}) %all-to-all-start) | async-done | bytes 3104 | tf_op jit(solution)/shard_map/all_to_all | solution.py:68
  257.6 1.1 fusion.32
  258.7 38.5 %psum.7 = f32[]{:T(128)} all-reduce(f32[]{:T(128)} %get-tuple-element.10), channel_id=1, replica_groups=mesh['dp'=4,'tensor'=8] {'dp','tensor'}, use_global_device_ids=true, to_apply=%region_16.17 | all-reduce | flops 1 | bytes 8 | tf_op jit(solution)/shard_map/psum | solution.py:79
  (7 shorter events, 0.1 us)
Async XLA Ops:
  7.2 105.1 %all-gather.2.cloned.1.call-start = ((), (), s32[]{:S(2)}) async-start(), calls=%async_computation.3 | async-start | bytes 7077888 | tf_op jit(solution)/shard_map/all_gather | solution.py:42
  11.8 3.1 %collective-permute-start = (bf16[512,1024]{1,0:T(8,128)(2,1)}, bf16[512,1024]{1,0:T(8,128)(2,1)}, u32[]{:S(2)}, u32[]{:S(2)}) collective-permute-start(bf16[512,1024]{1,0:T(8,128)(2,1)} %get-tuple-element.17), channel_id=1, source_target_pairs={{0,8},{8,0},{16,24},{24,16},{1,9},{9,1},{17,25},{25,17},{2,10},{10... | collective-permute-start | bytes 3145736 | tf_op jit(solution)/shard_map/ppermute | solution.py:13
  12.2 10.4 %collective-permute-start.4 = (bf16[512,1024]{1,0:T(8,128)(2,1)S(1)}, bf16[512,1024]{1,0:T(8,128)(2,1)}, u32[]{:S(2)}, u32[]{:S(2)}) collective-permute-start(bf16[512,1024]{1,0:T(8,128)(2,1)S(1)} %get-tuple-element.19), channel_id=1, source_target_pairs={{0,8},{8,0},{16,24},{24,16},{1,9},{9,1},{17,25},{25,17},{2,10},{10... | collective-permute-start | bytes 3145736 | tf_op jit(solution)/shard_map/ppermute | solution.py:13
  19.3 49.6 %collective-permute-start.1 = (bf16[512,2048]{1,0:T(8,128)(2,1)}, bf16[512,2048]{1,0:T(8,128)(2,1)}, u32[]{:S(2)}, u32[]{:S(2)}) collective-permute-start(bf16[512,2048]{1,0:T(8,128)(2,1)} %maximum_select_fusion.8), channel_id=1, source_target_pairs={{0,16},{8,24},{16,0},{24,8},{1,17},{9,25},{17,1},{25,9},{2,18},{10... | collective-permute-start | bytes 6291464 | tf_op jit(solution)/shard_map/ppermute | solution.py:13
  22.2 4.4 %collective-permute-start.6 = (bf16[512,1024]{1,0:T(8,128)(2,1)S(1)}, bf16[512,1024]{1,0:T(8,128)(2,1)}, u32[]{:S(2)}, u32[]{:S(2)}) collective-permute-start(bf16[512,1024]{1,0:T(8,128)(2,1)S(1)} %get-tuple-element.18), channel_id=1, source_target_pairs={{0,8},{8,0},{16,24},{24,16},{1,9},{9,1},{17,25},{25,17},{2,10},{10... | collective-permute-start | bytes 3145736 | tf_op jit(solution)/shard_map/ppermute | solution.py:13
  22.2 10.1 %collective-permute-start.2 = (bf16[512,1024]{1,0:T(8,128)(2,1)S(1)}, bf16[512,1024]{1,0:T(8,128)(2,1)}, u32[]{:S(2)}, u32[]{:S(2)}) collective-permute-start(bf16[512,1024]{1,0:T(8,128)(2,1)S(1)} %get-tuple-element.16), channel_id=1, source_target_pairs={{0,8},{8,0},{16,24},{24,16},{1,9},{9,1},{17,25},{25,17},{2,10},{10... | collective-permute-start | bytes 3145736 | tf_op jit(solution)/shard_map/ppermute | solution.py:13
  26.5 95.7 %collective-permute-start.5 = (bf16[512,2048]{1,0:T(8,128)(2,1)}, bf16[512,2048]{1,0:T(8,128)(2,1)}, u32[]{:S(2)}, u32[]{:S(2)}) collective-permute-start(bf16[512,2048]{1,0:T(8,128)(2,1)} %maximum_select_fusion.10), channel_id=1, source_target_pairs={{0,16},{8,24},{16,0},{24,8},{1,17},{9,25},{17,1},{25,9},{2,18},{10... | collective-permute-start | bytes 6291464 | tf_op jit(solution)/shard_map/ppermute | solution.py:13
  30.2 182.0 %collective-permute-start.7 = (bf16[512,2048]{1,0:T(8,128)(2,1)}, bf16[512,2048]{1,0:T(8,128)(2,1)}, u32[]{:S(2)}, u32[]{:S(2)}) collective-permute-start(bf16[512,2048]{1,0:T(8,128)(2,1)} %maximum_select_fusion.11), channel_id=1, source_target_pairs={{0,16},{8,24},{16,0},{24,8},{1,17},{9,25},{17,1},{25,9},{2,18},{10... | collective-permute-start | bytes 6291464 | tf_op jit(solution)/shard_map/ppermute | solution.py:13
  34.6 168.6 %collective-permute-start.3 = (bf16[512,2048]{1,0:T(8,128)(2,1)S(1)}, bf16[512,2048]{1,0:T(8,128)(2,1)}, u32[]{:S(2)}, u32[]{:S(2)}) collective-permute-start(bf16[512,2048]{1,0:T(8,128)(2,1)S(1)} %maximum_select_fusion.9), channel_id=1, source_target_pairs={{0,16},{8,24},{16,0},{24,8},{1,17},{9,25},{17,1},{25,9},{2,18},{10... | collective-permute-start | bytes 6291464 | tf_op jit(solution)/shard_map/ppermute | solution.py:13
  212.2 10.1 %copy-start = (f32[512,768]{1,0:T(8,128)S(1)}, f32[512,768]{1,0:T(8,128)}, u32[]{:S(2)}) copy-start(f32[512,768]{1,0:T(8,128)} %get-tuple-element.33) | copy-start | bytes 4718596
  212.2 10.1 %copy-start.1 = (f32[512,768]{1,0:T(8,128)S(1)}, f32[512,768]{1,0:T(8,128)}, u32[]{:S(2)}) copy-start(f32[512,768]{1,0:T(8,128)} %get-tuple-element.29) | copy-start | bytes 4718596
  212.2 10.1 %copy-start.2 = (s32[768]{0:T(1024)S(1)}, s32[768]{0:T(1024)}, u32[]{:S(2)}) copy-start(s32[768]{0:T(1024)} %param.5) | copy-start | bytes 9220
  226.4 12.6 %all-to-all-start.1 = ((f32[8,1,96]{2,1,0:T(1,128)}), f32[8,1,96]{2,1,0:T(1,128)S(1)}, u32[]{:S(2)}, u32[]{:S(2)}) async-start(f32[8,1,96]{2,1,0:T(1,128)} %bitcast.2), calls=%async_computation.1 | async-start | bytes 8192 | tf_op jit(solution)/shard_map/all_to_all | solution.py:65
  247.8 9.8 %all-to-all-start = ((f32[8,1,96]{2,1,0:T(1,128)}), f32[8,1,96]{2,1,0:T(1,128)S(1)}, u32[]{:S(2)}, u32[]{:S(2)}) async-start(f32[8,1,96]{2,1,0:T(1,128)} %bitcast), calls=%async_computation | async-start | bytes 8192 | tf_op jit(solution)/shard_map/all_to_all | solution.py:68
Sparse Core Ops, SparseCore 0:
  10.0 102.1 all-gather.1
